TPU v7x, 256 devices: a whole 4x4x8 slice. The times are simulated.
256 devices in a mesh: req: 2 (over core), row: 32 (over x, z), col: 4 (over y).
Axes of the slice: x: 4, y: 4, z: 8, core: 2. Of those that a mesh axis runs over, the one named last changes fastest.
Arguments:
- hidden: bfloat16 [2, 3072, 3072], P('req', 'row'), may hold values from -6 to 6
- text_hidden: bfloat16 [2, 128, 3072], P('req', 'row'), may hold values from -6 to 6
- text_len: int32 [2], replicated, may hold values from 32 to 128, as said below
- grid: int32 [2, 2], replicated, may hold values from 8 to 32, as said below
- timestep: int32 [2], replicated, may hold values from 250 to 999
- modulation: float32 [2, 8, 3072], P('req'), may hold values from -4 to 4
- q_gain: float32 [64], replicated, may hold values from 1 to 3
- k_gain: float32 [64], replicated, may hold values from 1 to 3
- w_qkv: bfloat16 [3, 3072, 3072], P(None, 'row', 'col'), may hold values from -0.109375 to 0.109375
- w_out: bfloat16 [3072, 3072], P('col'), may hold values from -0.109375 to 0.109375
- w_up: bfloat16 [3072, 12288], P(None, 'row'), may hold values from -0.109375 to 0.109375
- w_down: bfloat16 [12288, 3072], P('row'), may hold values from -0.0546875 to 0.0546875
- w_proj: bfloat16 [3072, 64], replicated, may hold values from -0.109375 to 0.109375
- latent: float32 [2, 3072, 64], P('req', ('row', 'col')), may hold values from -6 to 6
- conv_w: bfloat16 [3, 3, 16, 512], replicated, may hold values from -0.5 to 0.5
Outputs:
- hidden_out: bfloat16 [2, 3072, 3072], P('req', ('row', 'col'))
- new_latent: float32 [2, 3072, 64], P('req', ('row', 'col'))
- decoded: bfloat16 [2, 6, 64, 32, 512], P('req', None, 'row', 'col')
Inputs may be any that keep to these rules, and one draw needn't show every extreme that they name: Each request's live token rows and columns; one of the two requests, drawn, fills its whole grid of 32 rows and 16 columns, the other keeps at least half of each. `text_len`: one of the two requests, drawn, has all 128 text tokens live. The previous timestep of the sampling step is timestep - 250.
All inputs are finite; a program needn't handle non-finite values.
Results may differ from a plain program's by a relative error of at most 0.014.
Values may be sent and summed in bfloat16 or wider, within the bound.
A program may use at most 128 MiB of HBM per device.

v0:
```python
import jax
import jax.numpy as jnp
from jax import lax
from jax.sharding import PartitionSpec as P

CH = 16
FR = 6
TR = 1
TC = 4
TRAIN_STEPS = 1000
STRIDE = 250
latent_scale = 0.7


def extended(cells, sides, width):
    for axis, dim in sides:
        count = lax.axis_size(axis)
        ends = count - 1
        head = lax.slice_in_dim(cells, 0, width, axis=dim)
        tail = lax.slice_in_dim(cells, cells.shape[dim] - width, cells.shape[dim], axis=dim)
        cells = jnp.concatenate(
            [
                lax.ppermute(tail, axis, [(i, (i + 1) % count) for i in range(ends)]),
                cells,
                lax.ppermute(head, axis, [((i + 1) % count, i) for i in range(ends)]),
            ],
            axis=dim,
        )
    return cells


def layer_norm(tensor, epsilon):
    average = jnp.mean(tensor, axis=-1, keepdims=True)
    centered = tensor - average
    spread = jnp.mean(centered * centered, axis=-1, keepdims=True)
    return centered * lax.rsqrt(spread + epsilon)


def modulate(tensor, offset, factor):
    return (layer_norm(tensor, 1e-05) * (1.0 + factor) + offset).astype(jnp.bfloat16)


def head_norm(tensor, scaling):
    return (layer_norm(tensor, 1e-06) * scaling).astype(jnp.bfloat16)


def pick_entry(entries, position):
    slot_ids = jnp.arange(entries.shape[0], dtype=jnp.int32)
    return jnp.sum(jnp.where(slot_ids == position, entries, jnp.zeros_like(entries)))


def solver_weights(step_index):
    plan = jnp.linspace(0.00085**0.5, 0.012**0.5, TRAIN_STEPS, dtype=jnp.float32) ** 2
    cumulative = jnp.cumprod(1.0 - plan)
    alpha_now = pick_entry(cumulative, step_index)
    alpha_prev = pick_entry(cumulative, step_index - STRIDE)
    root_now = jnp.sqrt(alpha_now)
    rest_now = jnp.sqrt(1.0 - alpha_now)
    root_prev = jnp.sqrt(alpha_prev)
    rest_prev = jnp.sqrt(1.0 - alpha_prev)
    return (
        root_prev * root_now + rest_prev * rest_now,
        rest_prev * root_now - root_prev * rest_now,
    )


def key_mask(count, owners, grid, text_len, span, block_tokens, tile, text_rows):
    positions = jnp.arange(count, dtype=jnp.int32)
    owner_row = positions // span
    within = positions % span
    is_video = within < block_tokens
    owner_col = within // tile
    local_ids = within % tile
    token_row = owner_row * TR + local_ids // TC % TR
    token_col = owner_col * TC + local_ids % TC
    text_index = owner_row * text_rows + within - block_tokens
    matches = jnp.arange(grid.shape[0], dtype=jnp.int32)[None, :] == owners[:, None]
    rows_live = jnp.sum(jnp.where(matches, grid[None, :, 0], 0), axis=1)
    cols_live = jnp.sum(jnp.where(matches, grid[None, :, 1], 0), axis=1)
    text_lens = jnp.sum(jnp.where(matches, text_len[None, :], 0), axis=1)
    video_live = (token_row[None, :] < rows_live[:, None]) & (
        token_col[None, :] < cols_live[:, None]
    )
    text_live = text_index[None, :] < text_lens[:, None]
    return jnp.where(is_video[None, :], video_live, text_live).astype(jnp.float32)


def projector(stacked, piece):
    return jnp.einsum("gld,cde->cgle", stacked, piece, preferred_element_type=jnp.float32)


def attention_step(queries, owners, grid, text_len, span, block_tokens, tile, text_rows):
    score_scale = queries.shape[3] ** (-0.5)

    def attend(carry, pieces, start):
        key_piece, value_piece = pieces
        live_keys = key_mask(
            key_piece.shape[1], owners, grid, text_len, span, block_tokens, tile, text_rows
        )
        scores = (
            jnp.einsum("gqhd,gkhd->gqhk", queries, key_piece, preferred_element_type=jnp.float32)
            * score_scale
        )
        raw_weights = jnp.exp(scores) * live_keys[:, None, None, :]
        weighted = jnp.einsum(
            "gqhk,gkhd->gqhd",
            raw_weights.astype(jnp.bfloat16),
            value_piece,
            preferred_element_type=jnp.float32,
        )
        return (weighted, jnp.sum(raw_weights, axis=3))

    return attend


def shards(
    hidden,
    text_hidden,
    text_len,
    grid,
    timestep,
    modulation,
    q_gain,
    k_gain,
    w_qkv,
    w_out,
    w_up,
    w_down,
    w_proj,
    latent,
    conv_w,
):
    col_count = lax.axis_size("col")
    request_id = lax.axis_index("req")
    row_id = lax.axis_index("row")
    col_id = lax.axis_index("col")
    block_tokens = hidden.shape[1]
    tile = block_tokens // col_count
    text_rows = text_hidden.shape[1]
    head_dim = q_gain.shape[0]
    adaptive = modulation[0]
    source = hidden[0].astype(jnp.float32)
    joined = jnp.concatenate(
        [
            modulate(source, adaptive[0], adaptive[1]),
            modulate(text_hidden[0].astype(jnp.float32), adaptive[0], adaptive[1]),
        ],
        axis=0,
    )
    span = joined.shape[0]
    stacked = joined[None]
    owners = jnp.reshape(request_id, (1,))
    half_cols = w_qkv.shape[2] // 2
    own_half = lax.dynamic_slice_in_dim(w_qkv, request_id * half_cols, half_cols, 2)
    gathered_half = lax.all_gather(own_half, "row", axis=1, tiled=True)
    qkv = projector(stacked, lax.all_gather(gathered_half, "req", axis=2, tiled=True))
    groups = stacked.shape[0]
    heads_here = qkv.shape[3] // head_dim
    shaped = qkv.reshape(3, groups, span, heads_here, head_dim)
    queries = head_norm(shaped[0, :, :block_tokens], q_gain)
    key_block = head_norm(shaped[1], k_gain)
    value_block = shaped[2].astype(jnp.bfloat16)
    attend = attention_step(queries, owners, grid, text_len, span, block_tokens, tile, text_rows)
    empty_state = (jnp.zeros(queries.shape, jnp.float32), jnp.zeros(queries.shape[:3], jnp.float32))
    both = jnp.stack([key_block[0], value_block[0]], axis=0)[None]
    both = lax.all_gather(both, "row", axis=0, tiled=True)
    both = jnp.swapaxes(both, 0, 1).reshape(2, 1, -1, heads_here, head_dim)
    weighted, totals = attend(empty_state, (both[0], both[1]), jnp.int32(0))
    attended = (
        (weighted / totals[..., None])
        .astype(jnp.bfloat16)
        .reshape(groups * block_tokens, heads_here * head_dim)
    )
    partial_out = jnp.dot(attended, w_out, preferred_element_type=jnp.float32)
    projected = lax.psum_scatter(partial_out, "col", scatter_dimension=0, tiled=True)
    own_rows = lax.dynamic_slice_in_dim(source, col_id * tile, tile, 0)
    mixed = lax.optimization_barrier(
        (own_rows + adaptive[2] * projected).astype(jnp.bfloat16)
    ).astype(jnp.float32)
    second_norm = modulate(mixed, adaptive[3], adaptive[4])
    hidden_units = jax.nn.gelu(
        jnp.dot(
            lax.all_gather(second_norm, "row", axis=0, tiled=True),
            w_up,
            preferred_element_type=jnp.float32,
        ),
        approximate=True,
    ).astype(jnp.bfloat16)
    feed_terms = jnp.dot(hidden_units, w_down, preferred_element_type=jnp.float32)
    feed_out = lax.psum_scatter(
        feed_terms.astype(jnp.bfloat16), "row", scatter_dimension=0, tiled=True
    ).astype(jnp.float32)
    out_hidden = (mixed + adaptive[5] * feed_out).astype(jnp.bfloat16)
    final_norm = modulate(out_hidden.astype(jnp.float32), adaptive[6], adaptive[7])
    velocity = jnp.dot(final_norm, w_proj, preferred_element_type=jnp.float32)
    local_ids = jnp.arange(tile, dtype=jnp.int32)
    token_row = row_id * TR + local_ids // TC % TR
    token_col = col_id * TC + local_ids % TC
    rows_live = pick_entry(grid[:, 0], request_id)
    cols_live = pick_entry(grid[:, 1], request_id)
    live_tokens = ((token_row < rows_live) & (token_col < cols_live)).astype(jnp.float32)
    keep_part, velocity_part = solver_weights(pick_entry(timestep, request_id))
    updated = (keep_part * latent[0] + velocity_part * velocity) * live_tokens[:, None]
    pixels = (
        updated.reshape(FR, TR, TC, CH, 2, 2)
        .transpose(0, 1, 4, 2, 5, 3)
        .reshape(FR, 2 * TR, 2 * TC, CH)
    )
    scaled = (pixels / latent_scale).astype(jnp.bfloat16)
    padded = extended(scaled, (("row", 1), ("col", 2)), 1)
    running = jnp.zeros((FR, 2 * TR, 2 * TC, conv_w.shape[3]), jnp.float32)
    for row_tap in range(3):
        for col_tap in range(3):
            window = padded[:, row_tap : row_tap + 2 * TR, col_tap : col_tap + 2 * TC, :]
            running = running + jnp.einsum(
                "fyxc,cd->fyxd",
                window,
                conv_w[row_tap, col_tap],
                preferred_element_type=jnp.float32,
            )
    return (out_hidden[None], updated[None], running.astype(jnp.bfloat16)[None])


def solution(mesh):
    placed = (
        P("req", "row", None),
        P("req", "row", None),
        P(),
        P(),
        P(),
        P("req", None, None),
        P(),
        P(),
        P(None, "row", "col"),
        P("col", None),
        P(None, "row"),
        P("row", None),
        P(),
        P("req", ("row", "col"), None),
        P(),
    )
    return jax.shard_map(
        shards,
        mesh=mesh,
        in_specs=placed,
        out_specs=(
            P("req", ("row", "col"), None),
            P("req", ("row", "col"), None),
            P("req", None, "row", "col", None),
        ),
        check_vma=False,
    )
```

profile of v0, /device:TPU:26, one launch (start us, length us, event | category | flops | bytes accessed | tf_op | source)
XLA Modules:
  0.0 706.1 jit_solution(1297304816965305826)
XLA Ops:
  7.2 1.8 constant_dynamic-slice_fusion
  9.1 95.0 %all-gather.6.cloned.1.call-done = bf16[3,3072,384]{2,1,0:T(8,128)(2,1)} async-done(((bf16[3,96,384]{2,1,0:T(8,128)(2,1)}), bf16[3,3072,384]{2,1,0:T(8,128)(2,1)}) %all-gather.6.cloned.1.call-update) | async-done | bytes 7077904 | tf_op jit(solution)/shard_map/all_gather | solution.py:155
  107.4 28.7 %all-gather.8.cloned.1.call-done = bf16[3,3072,768]{2,1,0:T(8,128)(2,1)} async-done(((bf16[3,3072,384]{2,1,0:T(8,128)(2,1)}), bf16[3,3072,768]{2,1,0:T(8,128)(2,1)}) %all-gather.8.cloned.1.call-update) | async-done | bytes 14155792 | tf_op jit(solution)/shard_map/all_gather | solution.py:156
  136.1 7.0 convolution_bitcast_fusion
  147.3 2.0 fusion.152
  149.3 1.6 copy.32
  152.3 113.2 %all-gather.12.cloned.1.call-done = bf16[64,100,12,64]{1,3,2,0:T(8,128)(2,1)} async-done(((bf16[2,100,12,64]{1,3,2,0:T(8,128)(2,1)}), bf16[64,100,12,64]{1,3,2,0:T(8,128)(2,1)}) %all-gather.12.cloned.1.call-update) | async-done | bytes 9830416 | tf_op jit(solution)/shard_map/all_gather | solution.py:166
  265.5 11.9 %copy.45 = bf16[32,2,100,12,64]{2,0,4,3,1:T(8,128)(2,1)S(1)} copy(bf16[32,2,100,12,64]{2,4,3,1,0:T(8,128)(2,1)} %bitcast.213) | data formatting | bytes 19660800 | tf_op jit(solution)/shard_map/all_gather | solution.py:166
  277.4 5.5 fusion.175
  282.9 12.9 %reshape.413 = bf16[3200,12,64]{0,2,1:T(8,128)(2,1)} reshape(bf16[1,32,100,12,64]{2,1,4,3,0:T(8,128)(2,1)} %get-tuple-element.10) | data formatting | bytes 9830400 | tf_op jit(solution)/shard_map/reshape.45
  295.8 13.0 %reshape.414 = bf16[3200,12,64]{0,2,1:T(8,128)(2,1)} reshape(bf16[1,32,100,12,64]{2,1,4,3,0:T(8,128)(2,1)} %get-tuple-element.9) | data formatting | bytes 9830400 | tf_op jit(solution)/shard_map/reshape.37
  308.7 10.7 %bitcast_reduce_fusion = (f32[96,12]{0,1:T(8,128)S(1)}, f32[12,3200,96]{1,2,0:T(8,128)}) fusion(f32[3200]{0:T(1024)S(1)} %fusion.152, bf16[3200,12,64]{0,2,1:T(8,128)(2,1)} %reshape.414, f32[3,1,100,12,64]{2,4,3,0,1:T(8,128)} %bitcast.219, f32[64]{0:T(128)S(1)} %copy-done.23, f32[96,12]{0,1:T(8,128)S(1)} %copy-done.15, f32[96,12]{0,1:T(8,128)S(1)} %copy-done.10), kind=kOutput, calls=%fused_computation | convolution fusion | flops 483212160 | bytes 20080896 | tf_op jit(solution)/shard_map/gqhd,gkhd->gqhk/dot_general | solution.py:101
  319.4 8.3 %fusion.29 = bf16[1,96,12,64]{1,3,2,0:T(8,128)(2,1)S(1)} fusion(bf16[3200,12,64]{0,2,1:T(8,128)(2,1)S(1)} %bitcast.212, f32[12,3200,96]{1,2,0:T(8,128)} %get-tuple-element.24, f32[3200]{0:T(1024)S(1)} %fusion.152, f32[96,12]{0,1:T(8,128)S(1)} %get-tuple-element.23), kind=kOutput, calls=%fused_computation.37 | convolution fusion | flops 483065856 | bytes 19825664 | tf_op jit(solution)/shard_map/gqhk,gkhd->gqhd/dot_general | solution.py:105
  327.7 4.4 fusion.179
  333.3 22.0 %reduce-scatter.3.cloned.1.call-done = f32[24,3072]{1,0:T(8,128)} async-done(((f32[96,3072]{1,0:T(8,128)}), f32[24,3072]{1,0:T(8,128)}) %reduce-scatter.3.cloned.1.call-update) | async-done | bytes 294928 | tf_op jit(solution)/shard_map/reduce_scatter | solution.py:175
  357.9 84.8 %all-gather.10.cloned.1.call-done = bf16[768,3072]{1,0:T(8,128)(2,1)} async-done(((bf16[24,3072]{1,0:T(8,128)(2,1)}), bf16[768,3072]{1,0:T(8,128)(2,1)}) %all-gather.10.cloned.1.call-update) | async-done | bytes 4718608 | tf_op jit(solution)/shard_map/all_gather | solution.py:183
  442.7 10.4 %convolution_convert_fusion = bf16[768,3072]{1,0:T(8,128)(2,1)} fusion(bf16[384,3072]{1,0:T(8,128)(2,1)S(1)} %copy-done, bf16[768,3072]{1,0:T(8,128)(2,1)} %all-gather.10.cloned.1.call-done, bf16[3072,384]{1,0:T(8,128)(2,1)} %param.25), kind=kOutput, calls=%fused_computation.8 | convolution fusion | flops 3628892160 | bytes 14155776 | tf_op jit(solution)/shard_map/dot_general | solution.py:189
  461.0 213.4 %reduce-scatter.5.cloned.1.call-done = bf16[24,3072]{1,0:T(8,128)(2,1)} async-done(((bf16[768,3072]{1,0:T(8,128)(2,1)}), bf16[24,3072]{1,0:T(8,128)(2,1)}) %reduce-scatter.5.cloned.1.call-update) | async-done | bytes 147472 | tf_op jit(solution)/shard_map/reduce_scatter | solution.py:190
  677.1 4.5 collective-permute-start.1
  681.6 1.9 collective-permute-start
  683.7 5.6 collective-permute-done
  689.3 2.8 collective-permute-start.3
  692.1 1.3 collective-permute-start.2
  693.7 4.0 collective-permute-done.2
  (143 shorter events, 21.3 us)
Async XLA Ops:
  7.2 435.5 %copy-start = (bf16[384,3072]{1,0:T(8,128)(2,1)S(1)}, bf16[384,3072]{1,0:T(8,128)(2,1)}, u32[]{:S(2)}) copy-start(bf16[384,3072]{1,0:T(8,128)(2,1)} %param.26) | copy-start | bytes 7077892
  7.2 96.9 %all-gather.6.cloned.1.call-start = ((), (), s32[]{:S(2)}) async-start(), calls=%async_computation.2 | async-start | bytes 7299072 | tf_op jit(solution)/shard_map/all_gather | solution.py:155
  9.0 127.1 %all-gather.8.cloned.1.call-start = ((), (), s32[]{:S(2)}) async-start(), calls=%async_computation.3 | async-start | bytes 21233664 | tf_op jit(solution)/shard_map/all_gather | solution.py:156
  104.1 161.4 %all-gather.12.cloned.1.call-start = ((), (), s32[]{:S(2)}) async-start(), calls=%async_computation.7 | async-start | bytes 12976128 | tf_op jit(solution)/shard_map/all_gather | solution.py:166
  145.7 209.6 %reduce-scatter.3.cloned.1.call-start = ((), (), s32[]{:S(2)}) async-start(), calls=%async_computation.4 | async-start | bytes 1474560 | tf_op jit(solution)/shard_map/reduce_scatter | solution.py:175
  150.9 126.5 %copy-start.3 = (f32[3,1,100,768]{2,3,0,1:T(8,128)}, f32[3,1,100,768]{2,3,0,1:T(8,128)S(1)}, u32[]{:S(2)}) copy-start(f32[3,1,100,768]{2,3,0,1:T(8,128)S(1)} %copy.32) | copy-start | bytes 2764804
  295.8 13.0 %copy-start.23 = (f32[64]{0:T(128)S(1)}, f32[64]{0:T(128)}, u32[]{:S(2)}) copy-start(f32[64]{0:T(128)} %param.21) | copy-start | bytes 772
  295.8 23.6 %slice-start = ((s8[4915200]{0:T(1024)(128)(4,1)}), s8[720896]{0:T(1024)(128)(4,1)S(1)}, s32[]{:S(2)}) async-start(s8[4915200]{0:T(1024)(128)(4,1)} %bitcast.211), calls=%async_computation.8 | async-start | bytes 1441792
  332.1 23.2 %copy-start.14 = (f32[1,1,3072]{2,1,0:T(1,128)S(1)}, f32[1,1,3072]{2,1,0:T(1,128)}, u32[]{:S(2)}) copy-start(f32[1,1,3072]{2,1,0:T(1,128)} %get-tuple-element.17) | copy-start | bytes 36868
  332.1 24.6 %copy-start.11 = (f32[1,1,3072]{2,1,0:T(1,128)S(1)}, f32[1,1,3072]{2,1,0:T(1,128)}, u32[]{:S(2)}) copy-start(f32[1,1,3072]{2,1,0:T(1,128)} %get-tuple-element.12) | copy-start | bytes 36868
  332.1 24.7 %copy-start.12 = (f32[1,1,3072]{2,1,0:T(1,128)S(1)}, f32[1,1,3072]{2,1,0:T(1,128)}, u32[]{:S(2)}) copy-start(f32[1,1,3072]{2,1,0:T(1,128)} %get-tuple-element.13) | copy-start | bytes 36868
  332.1 110.5 %all-gather.10.cloned.1.call-start = ((), (), s32[]{:S(2)}) async-start(), calls=%async_computation.5 | async-start | bytes 4866048 | tf_op jit(solution)/shard_map/all_gather | solution.py:183
  357.6 316.7 %reduce-scatter.5.cloned.1.call-start = ((), (), s32[]{:S(2)}) async-start(), calls=%async_computation.6 | async-start | bytes 4866048 | tf_op jit(solution)/shard_map/reduce_scatter | solution.py:190
  453.0 221.3 %copy-start.13 = (f32[1,1,3072]{2,1,0:T(1,128)S(1)}, f32[1,1,3072]{2,1,0:T(1,128)}, u32[]{:S(2)}) copy-start(f32[1,1,3072]{2,1,0:T(1,128)} %get-tuple-element.14) | copy-start | bytes 36868
  453.1 222.6 %copy-start.16 = (f32[1,1,3072]{2,1,0:T(1,128)S(1)}, f32[1,1,3072]{2,1,0:T(1,128)}, u32[]{:S(2)}) copy-start(f32[1,1,3072]{2,1,0:T(1,128)} %get-tuple-element.11) | copy-start | bytes 36868
  453.1 222.6 %copy-start.17 = (f32[1,1,3072]{2,1,0:T(1,128)S(1)}, f32[1,1,3072]{2,1,0:T(1,128)}, u32[]{:S(2)}) copy-start(f32[1,1,3072]{2,1,0:T(1,128)} %get-tuple-element.18) | copy-start | bytes 36868
  453.1 222.6 %copy-start.26 = (bf16[3072,64]{0,1:T(8,128)(2,1)S(1)}, bf16[3072,64]{0,1:T(8,128)(2,1)}, u32[]{:S(2)}) copy-start(bf16[3072,64]{0,1:T(8,128)(2,1)} %param.27) | copy-start | bytes 1179652
  453.1 222.6 %copy-start.27 = (f32[1,24,64]{2,1,0:T(8,128)S(1)}, f32[1,24,64]{2,1,0:T(8,128)}, u32[]{:S(2)}) copy-start(f32[1,24,64]{2,1,0:T(8,128)} %param.28) | copy-start | bytes 18436
  453.1 230.4 %copy-start.7 = (bf16[3,3,16,512]{3,2,1,0:T(8,128)(2,1)S(1)}, bf16[3,3,16,512]{3,2,1,0:T(8,128)(2,1)}, u32[]{:S(2)}) copy-start(bf16[3,3,16,512]{3,2,1,0:T(8,128)(2,1)} %param.29) | copy-start | bytes 442372
  675.4 23.8 %copy-start.5 = (bf16[24,3072]{1,0:T(8,128)(2,1)}, bf16[24,3072]{1,0:T(8,128)(2,1)S(1)}, u32[]{:S(2)}) copy-start(bf16[24,3072]{1,0:T(8,128)(2,1)S(1)} %get-tuple-element.8) | copy-start | bytes 442372
  677.1 6.6 collective-permute-start.1
  681.6 7.7 %collective-permute-start = (bf16[6,1,8,16]{3,2,1,0:T(8,128)(2,1)S(1)}, bf16[6,1,8,16]{3,2,1,0:T(8,128)(2,1)S(1)}, u32[]{:S(2)}, u32[]{:S(2)}) collective-permute-start(bf16[6,1,8,16]{3,2,1,0:T(8,128)(2,1)S(1)} %get-tuple-element.21), channel_id=1, source_target_pairs={{0,4},{4,8},{8,12},{12,16},{16,20},{20,24},{24,28},{28,32},{32,36}... | collective-permute-start | bytes 4616 | tf_op jit(solution)/shard_map/ppermute | solution.py:23
  689.3 8.7 %collective-permute-start.3 = (bf16[6,4,1,16]{3,2,1,0:T(2,128)(2,1)S(1)}, bf16[6,4,1,16]{3,2,1,0:T(2,128)(2,1)S(1)}, u32[]{:S(2)}, u32[]{:S(2)}) collective-permute-start(bf16[6,4,1,16]{3,2,1,0:T(2,128)(2,1)S(1)} %get-tuple-element.20), channel_id=1, source_target_pairs={{1,0},{2,1},{3,2},{5,4},{6,5},{7,6},{9,8},{10,9},{11,10},{13,12},{... | collective-permute-start | bytes 2312 | tf_op jit(solution)/shard_map/ppermute | solution.py:25
  692.1 5.6 collective-permute-start.2
  (17 other events, 63.0 us)
Sparse Core Ops, SparseCore 0:
  10.6 93.4 all-gather.5
  105.9 30.1 all-gather.7
  145.8 119.6 all-gather.11
  332.3 22.9 reduce-scatter.2
  358.3 84.3 all-gather.9
  453.3 221.0 reduce-scatter.4
where the time goes:
time: 707 us; the launch traced here: 706 us
  waiting for transfers between devices  567 us (80%)
  local copies, waits for them, and re-layouts  50.3 us (7%)
  matrix products  43.7 us (6%)
  between operations  18.5 us (3%)
  other arithmetic  16 us (2%)
  starting transfers between devices  10.9 us (2%)
    reduce_scatter x1, waiting for transfers between devices, shards(): lax.psum_scatter(feed_terms.astype(jnp.bfloat16), 'row', scatter_dimensio...  213 us
    all_gather x1, waiting for transfers between devices, shards(): both = lax.all_gather(both, 'row', axis=0, tiled=True)  113 us
    all_gather x1, waiting for transfers between devices, shards(): gathered_half = lax.all_gather(own_half, 'row', axis=1, tiled=True)  95 us
    all_gather x1, waiting for transfers between devices, shards(): lax.all_gather(second_norm, 'row', axis=0, tiled=True)  84.8 us
    all_gather x1, waiting for transfers between devices, shards(): lax.all_gather(gathered_half, 'req', axis=2, tiled=True)  28.7 us
    another operation x4, local copies, waits for them, and re-layouts  26 us
    reduce_scatter x1, waiting for transfers between devices, shards(): lax.psum_scatter(partial_out, 'col', scatter_dimension=0, tiled=True)  22 us
  transfers between devices with their start and end apart: 10, of which 8 were waited for; matrix products, arithmetic and copies ran while one was open for 2% of the time, Pallas kernels for 0%

commit v1 on v0

--- a/solution.py
+++ b/solution.py
@@ -180,7 +180,9 @@
     second_norm = modulate(mixed, adaptive[3], adaptive[4])
     hidden_units = jax.nn.gelu(
         jnp.dot(
-            lax.all_gather(second_norm, "row", axis=0, tiled=True),
+            jnp.concatenate(
+                lax.all_to_all(jnp.stack([second_norm] * lax.axis_size("row")), "row", 0, 0), axis=0
+            ),
             w_up,
             preferred_element_type=jnp.float32,
         ),

time: 707 us -> 736 us (1.041)
  blocking collectives: 0 us -> 115 us
  waiting for transfers between devices: 567 us -> 482 us
    all_to_all x0 -> x1, blocking collectives: none -> 115 us  [shards(): lax.all_to_all(jnp.stack([second_norm] * lax.axis_size('row')), 'row', 0, 0)]
    all_gather x1 -> x0, waiting for transfers between devices: 84.8 us -> none  [shards(): lax.all_gather(second_norm, 'row', axis=0, tiled=True)]
    another operation x4 -> x5, local copies, waits for them, and re-layouts: 26 us -> 26.5 us
  transfers between devices with their start and end apart: 10 -> 9, of which waited for: 8 -> 7; matrix products, arithmetic and copies ran while one was open for 2% -> 2% of each run, Pallas kernels for 0% -> 0%
where the time goes in v1:
time: 736 us; the launch traced here: 735 us
  waiting for transfers between devices  482 us (65%)
  blocking collectives  115 us (16%)
  local copies, waits for them, and re-layouts  50.3 us (7%)
  matrix products  43.6 us (6%)
  between operations  18.2 us (2%)
  other arithmetic  15.4 us (2%)
  starting transfers between devices  11 us (1%)
    reduce_scatter x1, waiting for transfers between devices, shards(): lax.psum_scatter(feed_terms.astype(jnp.bfloat16), 'row', scatter_dimensio...  213 us
    all_to_all x1, blocking collectives, shards(): lax.all_to_all(jnp.stack([second_norm] * lax.axis_size('row')), 'row', 0, 0)  115 us
    all_gather x1, waiting for transfers between devices, shards(): both = lax.all_gather(both, 'row', axis=0, tiled=True)  113 us
    all_gather x1, waiting for transfers between devices, shards(): gathered_half = lax.all_gather(own_half, 'row', axis=1, tiled=True)  95 us
    all_gather x1, waiting for transfers between devices, shards(): lax.all_gather(gathered_half, 'req', axis=2, tiled=True)  29.3 us
    another operation x4, local copies, waits for them, and re-layouts  26 us
    reduce_scatter x1, waiting for transfers between devices, shards(): lax.psum_scatter(partial_out, 'col', scatter_dimension=0, tiled=True)  21.7 us
  transfers between devices with their start and end apart: 9, of which 7 were waited for; matrix products, arithmetic and copies ran while one was open for 2% of the time, Pallas kernels for 0%

profile of v1, /device:TPU:26, one launch (start us, length us, event | category | flops | bytes accessed | tf_op | source)
XLA Modules:
  0.0 734.9 jit_solution(14316434215863838945)
XLA Ops:
  7.3 1.8 constant_dynamic-slice_fusion
  9.1 95.0 %all-gather.5.cloned.1.call-done = bf16[3,3072,384]{2,1,0:T(8,128)(2,1)} async-done(((bf16[3,96,384]{2,1,0:T(8,128)(2,1)}), bf16[3,3072,384]{2,1,0:T(8,128)(2,1)}) %all-gather.5.cloned.1.call-update) | async-done | bytes 7077904 | tf_op jit(solution)/shard_map/all_gather | solution.py:155
  106.8 29.3 %all-gather.7.cloned.1.call-done = bf16[3,3072,768]{2,1,0:T(8,128)(2,1)} async-done(((bf16[3,3072,384]{2,1,0:T(8,128)(2,1)}), bf16[3,3072,768]{2,1,0:T(8,128)(2,1)}) %all-gather.7.cloned.1.call-update) | async-done | bytes 14155792 | tf_op jit(solution)/shard_map/all_gather | solution.py:156
  136.1 7.0 convolution_bitcast_fusion
  147.3 2.0 fusion.152
  149.3 1.6 copy.32
  152.3 113.2 %all-gather.9.cloned.1.call-done = bf16[64,100,12,64]{1,3,2,0:T(8,128)(2,1)} async-done(((bf16[2,100,12,64]{1,3,2,0:T(8,128)(2,1)}), bf16[64,100,12,64]{1,3,2,0:T(8,128)(2,1)}) %all-gather.9.cloned.1.call-update) | async-done | bytes 9830416 | tf_op jit(solution)/shard_map/all_gather | solution.py:166
  265.5 11.9 %copy.45 = bf16[32,2,100,12,64]{2,0,4,3,1:T(8,128)(2,1)S(1)} copy(bf16[32,2,100,12,64]{2,4,3,1,0:T(8,128)(2,1)} %bitcast.214) | data formatting | bytes 19660800 | tf_op jit(solution)/shard_map/all_gather | solution.py:166
  277.4 5.5 fusion.175
  282.9 12.9 %reshape.418 = bf16[3200,12,64]{0,2,1:T(8,128)(2,1)} reshape(bf16[1,32,100,12,64]{2,1,4,3,0:T(8,128)(2,1)} %get-tuple-element.10) | data formatting | bytes 9830400 | tf_op jit(solution)/shard_map/reshape.46
  295.8 13.0 %reshape.419 = bf16[3200,12,64]{0,2,1:T(8,128)(2,1)} reshape(bf16[1,32,100,12,64]{2,1,4,3,0:T(8,128)(2,1)} %get-tuple-element.9) | data formatting | bytes 9830400 | tf_op jit(solution)/shard_map/reshape.38
  308.8 10.7 %bitcast_reduce_fusion = (f32[96,12]{0,1:T(8,128)S(1)}, f32[12,3200,96]{1,2,0:T(8,128)}) fusion(f32[3200]{0:T(1024)S(1)} %fusion.152, bf16[3200,12,64]{0,2,1:T(8,128)(2,1)} %reshape.419, f32[3,1,100,12,64]{2,4,3,0,1:T(8,128)} %bitcast.221, f32[64]{0:T(128)S(1)} %copy-done.23, f32[96,12]{0,1:T(8,128)S(1)} %copy-done.15, f32[96,12]{0,1:T(8,128)S(1)} %copy-done.10), kind=kOutput, calls=%fused_computation | convolution fusion | flops 483212160 | bytes 20080896 | tf_op jit(solution)/shard_map/gqhd,gkhd->gqhk/dot_general | solution.py:101
  319.4 8.3 %fusion.29 = bf16[1,96,12,64]{1,3,2,0:T(8,128)(2,1)S(1)} fusion(bf16[3200,12,64]{0,2,1:T(8,128)(2,1)S(1)} %bitcast.213, f32[12,3200,96]{1,2,0:T(8,128)} %get-tuple-element.24, f32[3200]{0:T(1024)S(1)} %fusion.152, f32[96,12]{0,1:T(8,128)S(1)} %get-tuple-element.23), kind=kOutput, calls=%fused_computation.37 | convolution fusion | flops 483065856 | bytes 19825664 | tf_op jit(solution)/shard_map/gqhk,gkhd->gqhd/dot_general | solution.py:105
  327.8 4.4 fusion.179
  333.6 21.7 %reduce-scatter.3.cloned.1.call-done = f32[24,3072]{1,0:T(8,128)} async-done(((f32[96,3072]{1,0:T(8,128)}), f32[24,3072]{1,0:T(8,128)}) %reduce-scatter.3.cloned.1.call-update) | async-done | bytes 294928 | tf_op jit(solution)/shard_map/reduce_scatter | solution.py:175
  357.5 114.9 %all_to_all.5 = bf16[32,24,3072]{2,1,0:T(8,128)(2,1)} all-to-all(bf16[32,24,3072]{2,1,0:T(8,128)(2,1)S(1)} %stack.5), channel_id=1, replica_groups=mesh['req'=2,'row'=32,'col'=4] {'row'}, dimensions={0} | all-to-all | bytes 9437184 | tf_op jit(solution)/shard_map/all_to_all | solution.py:184
  472.4 10.4 %convolution_convert_fusion = bf16[768,3072]{1,0:T(8,128)(2,1)} fusion(bf16[384,3072]{1,0:T(8,128)(2,1)S(1)} %copy-done, bf16[768,3072]{1,0:T(8,128)(2,1)} %bitcast.218, bf16[3072,384]{1,0:T(8,128)(2,1)} %param.25), kind=kOutput, calls=%fused_computation.8 | convolution fusion | flops 3628892160 | bytes 14155776 | tf_op jit(solution)/shard_map/dot_general | solution.py:191
  490.7 212.6 %reduce-scatter.5.cloned.1.call-done = bf16[24,3072]{1,0:T(8,128)(2,1)} async-done(((bf16[768,3072]{1,0:T(8,128)(2,1)}), bf16[24,3072]{1,0:T(8,128)(2,1)}) %reduce-scatter.5.cloned.1.call-update) | async-done | bytes 147472 | tf_op jit(solution)/shard_map/reduce_scatter | solution.py:192
  706.1 4.6 collective-permute-start.1
  710.7 1.9 collective-permute-start
  712.8 5.6 collective-permute-done
  718.4 2.8 collective-permute-start.3
  721.2 1.3 collective-permute-start.2
  722.8 4.0 collective-permute-done.2
  (142 shorter events, 20.5 us)
Async XLA Ops:
  7.2 465.2 %copy-start = (bf16[384,3072]{1,0:T(8,128)(2,1)S(1)}, bf16[384,3072]{1,0:T(8,128)(2,1)}, u32[]{:S(2)}) copy-start(bf16[384,3072]{1,0:T(8,128)(2,1)} %param.26) | copy-start | bytes 7077892
  7.2 97.0 %copy-start.6 = (bf16[1,4,3072]{2,1,0:T(4,128)(2,1)S(1)}, bf16[1,4,3072]{2,1,0:T(4,128)(2,1)}, u32[]{:S(2)}) copy-start(bf16[1,4,3072]{2,1,0:T(4,128)(2,1)} %param.16) | copy-start | bytes 73732
  7.2 97.4 %copy-start.1 = (bf16[1,96,3072]{2,1,0:T(8,128)(2,1)S(1)}, bf16[1,96,3072]{2,1,0:T(8,128)(2,1)}, u32[]{:S(2)}) copy-start(bf16[1,96,3072]{2,1,0:T(8,128)(2,1)} %param.15) | copy-start | bytes 1769476
  7.2 97.9 %copy-start.8 = (f32[1,8,3072]{2,1,0:T(8,128)S(1)}, f32[1,8,3072]{2,1,0:T(8,128)}, u32[]{:S(2)}) copy-start(f32[1,8,3072]{2,1,0:T(8,128)} %param.20) | copy-start | bytes 294916
  7.2 96.9 %all-gather.5.cloned.1.call-start = ((), (), s32[]{:S(2)}) async-start(), calls=%async_computation.3 | async-start | bytes 7299072 | tf_op jit(solution)/shard_map/all_gather | solution.py:155
  9.1 127.1 %all-gather.7.cloned.1.call-start = ((), (), s32[]{:S(2)}) async-start(), calls=%async_computation.4 | async-start | bytes 21233664 | tf_op jit(solution)/shard_map/all_gather | solution.py:156
  104.1 161.4 %all-gather.9.cloned.1.call-start = ((), (), s32[]{:S(2)}) async-start(), calls=%async_computation.7 | async-start | bytes 12976128 | tf_op jit(solution)/shard_map/all_gather | solution.py:166
  106.8 37.9 %copy-start.25 = (f32[64]{0:T(128)S(1)}, f32[64]{0:T(128)}, u32[]{:S(2)}) copy-start(f32[64]{0:T(128)} %param.22) | copy-start | bytes 772
  106.8 39.0 %copy-start.28 = (s32[2]{0:T(128)S(1)}, s32[2]{0:T(128)}, u32[]{:S(2)}) copy-start(s32[2]{0:T(128)} %param.17) | copy-start | bytes 28
  106.8 39.6 %copy-start.20 = (s32[2,2]{1,0:T(2,128)S(1)}, s32[2,2]{1,0:T(2,128)}, u32[]{:S(2)}) copy-start(s32[2,2]{1,0:T(2,128)} %param.18) | copy-start | bytes 52
  145.7 209.6 %reduce-scatter.3.cloned.1.call-start = ((), (), s32[]{:S(2)}) async-start(), calls=%async_computation.5 | async-start | bytes 1474560 | tf_op jit(solution)/shard_map/reduce_scatter | solution.py:175
  150.9 126.5 %copy-start.3 = (f32[3,1,100,768]{2,3,0,1:T(8,128)}, f32[3,1,100,768]{2,3,0,1:T(8,128)S(1)}, u32[]{:S(2)}) copy-start(f32[3,1,100,768]{2,3,0,1:T(8,128)S(1)} %copy.32) | copy-start | bytes 2764804
  327.8 29.0 %copy-start.11 = (f32[1,1,3072]{2,1,0:T(1,128)S(1)}, f32[1,1,3072]{2,1,0:T(1,128)}, u32[]{:S(2)}) copy-start(f32[1,1,3072]{2,1,0:T(1,128)} %get-tuple-element.12) | copy-start | bytes 36868
  332.2 371.1 %reduce-scatter.5.cloned.1.call-start = ((), (), s32[]{:S(2)}) async-start(), calls=%async_computation.6 | async-start | bytes 4866048 | tf_op jit(solution)/shard_map/reduce_scatter | solution.py:192
  482.8 220.6 %copy-start.13 = (f32[1,1,3072]{2,1,0:T(1,128)S(1)}, f32[1,1,3072]{2,1,0:T(1,128)}, u32[]{:S(2)}) copy-start(f32[1,1,3072]{2,1,0:T(1,128)} %get-tuple-element.14) | copy-start | bytes 36868
  482.8 221.9 %copy-start.16 = (f32[1,1,3072]{2,1,0:T(1,128)S(1)}, f32[1,1,3072]{2,1,0:T(1,128)}, u32[]{:S(2)}) copy-start(f32[1,1,3072]{2,1,0:T(1,128)} %get-tuple-element.11) | copy-start | bytes 36868
  482.8 221.9 %copy-start.17 = (f32[1,1,3072]{2,1,0:T(1,128)S(1)}, f32[1,1,3072]{2,1,0:T(1,128)}, u32[]{:S(2)}) copy-start(f32[1,1,3072]{2,1,0:T(1,128)} %get-tuple-element.18) | copy-start | bytes 36868
  482.8 221.9 %copy-start.26 = (bf16[3072,64]{0,1:T(8,128)(2,1)S(1)}, bf16[3072,64]{0,1:T(8,128)(2,1)}, u32[]{:S(2)}) copy-start(bf16[3072,64]{0,1:T(8,128)(2,1)} %param.27) | copy-start | bytes 1179652
  482.8 221.9 %copy-start.27 = (f32[1,24,64]{2,1,0:T(8,128)S(1)}, f32[1,24,64]{2,1,0:T(8,128)}, u32[]{:S(2)}) copy-start(f32[1,24,64]{2,1,0:T(8,128)} %param.28) | copy-start | bytes 18436
  482.8 229.8 %copy-start.7 = (bf16[3,3,16,512]{3,2,1,0:T(8,128)(2,1)S(1)}, bf16[3,3,16,512]{3,2,1,0:T(8,128)(2,1)}, u32[]{:S(2)}) copy-start(bf16[3,3,16,512]{3,2,1,0:T(8,128)(2,1)} %param.29) | copy-start | bytes 442372
  706.1 6.7 collective-permute-start.1
  710.7 7.7 %collective-permute-start = (bf16[6,1,8,16]{3,2,1,0:T(8,128)(2,1)S(1)}, bf16[6,1,8,16]{3,2,1,0:T(8,128)(2,1)S(1)}, u32[]{:S(2)}, u32[]{:S(2)}) collective-permute-start(bf16[6,1,8,16]{3,2,1,0:T(8,128)(2,1)S(1)} %get-tuple-element.21), channel_id=1, source_target_pairs={{0,4},{4,8},{8,12},{12,16},{16,20},{20,24},{24,28},{28,32},{32,36}... | collective-permute-start | bytes 4616 | tf_op jit(solution)/shard_map/ppermute | solution.py:23
  718.4 8.7 %collective-permute-start.3 = (bf16[6,4,1,16]{3,2,1,0:T(2,128)(2,1)S(1)}, bf16[6,4,1,16]{3,2,1,0:T(2,128)(2,1)S(1)}, u32[]{:S(2)}, u32[]{:S(2)}) collective-permute-start(bf16[6,4,1,16]{3,2,1,0:T(2,128)(2,1)S(1)} %get-tuple-element.20), channel_id=1, source_target_pairs={{1,0},{2,1},{3,2},{5,4},{6,5},{7,6},{9,8},{10,9},{11,10},{13,12},{... | collective-permute-start | bytes 2312 | tf_op jit(solution)/shard_map/ppermute | solution.py:25
  721.2 5.6 collective-permute-start.2
  (16 other events, 169.6 us)
Sparse Core Ops, SparseCore 0:
  10.6 93.4 all-gather.4
  105.9 30.1 all-gather.6
  145.8 119.6 all-gather.8
  332.3 22.9 reduce-scatter.2
  483.0 220.3 reduce-scatter.4
